TPU v7x, 32 devices: a whole 2x2x4 slice. The times are simulated.
32 devices in a mesh: row: 4 (over x, core), col: 8 (over z, y).
Axes of the slice: x: 2, y: 2, z: 4, core: 2. Of those that a mesh axis runs over, the one named last changes fastest.
Arguments:
- adjacency_tiles: bfloat16 [4, 8, 80, 128, 128], P('row', 'col'), may hold values from -0.09375 to 0.09375
- tile_rows: int32 [4, 8, 80], P('row', 'col'), may hold values from 0 to 15, as said below
- tile_cols: int32 [4, 8, 80], P('row', 'col'), may hold values from 0 to 7, as said below
- tile_counts: int32 [4, 8], P('row', 'col'), may hold values from 40 to 80, as said below
- features: bfloat16 [8192, 1024], P('col', 'row'), may hold values from -6 to 6
- weight: bfloat16 [1024, 1024], P('col'), may hold values from -0.1875 to 0.1875
Outputs:
- activated: bfloat16 [8192, 1024], P(('row', 'col'))
Inputs may be any that keep to these rules, and one draw needn't show every extreme that they name: `tile_counts`: some grid cell holds exactly 80 live tiles in every draw. In each grid cell the first tile_counts entries of tile_rows and tile_cols name distinct (row, column) tile pairs; later entries are valid indices but unused. `tile_cols`: see tile_rows.
All inputs are finite; a program needn't handle non-finite values.
Results may differ from a plain program's by a relative error of at most 0.014.
Values may be sent and summed in bfloat16 or wider, within the bound.
A program may use at most 64 MiB of HBM per device.

v0:
```python
import jax
import jax.numpy as jnp
from jax import lax
from jax.sharding import PartitionSpec as P


def densify(adjacency_tiles, tile_rows, tile_cols, tile_count, row_blocks, column_blocks):
    slots = adjacency_tiles.shape[0]
    tile_edge = adjacency_tiles.shape[1]
    live_mask = (jnp.arange(slots, dtype=jnp.int32) < tile_count).astype(jnp.bfloat16)
    masked = adjacency_tiles * live_mask[:, None, None]
    grid = jnp.zeros((row_blocks, column_blocks, tile_edge, tile_edge), jnp.bfloat16)
    grid = grid.at[tile_rows, tile_cols].add(masked)
    return grid.transpose(0, 2, 1, 3).reshape(row_blocks * tile_edge, column_blocks * tile_edge)


def reduce_whole(partial_rows):
    return lax.psum_scatter(
        partial_rows.astype(jnp.bfloat16), "col", scatter_dimension=0, tiled=True
    ).astype(jnp.float32)


def shards(adjacency_tiles, tile_rows, tile_cols, tile_counts, features, weight):
    local_tiles = adjacency_tiles[0, 0]
    local_rows = tile_rows[0, 0]
    local_cols = tile_cols[0, 0]
    local_count = tile_counts[0, 0]
    tile_edge = local_tiles.shape[1]
    column_blocks = features.shape[0] // tile_edge
    row_blocks = column_blocks * lax.axis_size("col") // lax.axis_size("row")
    dense_block = densify(
        local_tiles, local_rows, local_cols, local_count, row_blocks, column_blocks
    )
    whole = lax.all_gather(features, "row", axis=1, tiled=True)
    partial_value = jnp.dot(dense_block, whole, preferred_element_type=jnp.float32)
    summed = reduce_whole(partial_value.astype(jnp.bfloat16).astype(jnp.float32))
    aggregated = summed.astype(jnp.bfloat16)
    full_weight = lax.all_gather(weight, "col", axis=0, tiled=True)
    hidden = jnp.dot(aggregated, full_weight, preferred_element_type=jnp.float32)
    return jnp.maximum(hidden, 0.0).astype(jnp.bfloat16)


def solution(mesh):
    return jax.shard_map(
        shards,
        mesh=mesh,
        in_specs=(
            P("row", "col", None, None, None),
            P("row", "col", None),
            P("row", "col", None),
            P("row", "col"),
            P("col", "row"),
            P("col", None),
        ),
        out_specs=P(("row", "col"), None),
        check_vma=False,
    )
```

profile of v0, /device:TPU:0, one launch (start us, length us, event | category | flops | bytes accessed | tf_op | source)
XLA Modules:
  0.0 185.9 jit_solution(528085038853314362)
XLA Ops:
  6.5 0.0 all-gather.3.cloned.1.call-start
  6.5 0.7 all-gather.3.cloned.1.call-update
  7.3 0.0 all-gather.5.cloned.1.call-start
  7.3 0.7 all-gather.5.cloned.1.call-update
  8.0 0.0 reduce-scatter.2.cloned.1.call-start
  8.7 0.7 fusion.8
  9.4 2.0 %bitcast_multiply_fusion = bf16[80,128,128]{2,1,0:T(8,128)(2,1)S(1)} fusion(bf16[1,1,80,128,128]{4,3,2,1,0:T(8,128)(2,1)} %param.6, bf16[80]{0:T(256)(128)(2,1)S(1)} %compare_convert_fusion), kind=kLoop, calls=%fused_computation.5 | loop fusion | flops 1310720 | bytes 5243040 | tf_op jit(solution)/shard_map/mul | solution.py:11
  11.4 3.0 %broadcast_in_dim.2 = bf16[16,8,128,128]{3,2,1,0:T(8,128)(2,1)} broadcast(bf16[]{:T(256)} %constant.0.clone.1), dimensions={} | broadcast | bytes 4194306 | tf_op jit(solution)/shard_map/broadcast_in_dim | solution.py:12
  14.4 15.4 %scatter_fusion = bf16[16,8,128,128]{3,2,1,0:T(8,128)(2,1)} fusion(bf16[16,8,128,128]{3,2,1,0:T(8,128)(2,1)} %broadcast_in_dim.2, s32[80]{0:T(128)S(1)} %fusion.8, bf16[80,128,128]{2,1,0:T(8,128)(2,1)S(1)} %bitcast_multiply_fusion), kind=kCustom, calls=%fused_computation | custom fusion | flops 1310720 | bytes 7864960 | tf_op jit(solution)/shard_map/scatter-add | solution.py:13
  29.8 7.7 %copy.7 = bf16[16,128,8,128]{3,2,1,0:T(8,128)(2,1)} copy(bf16[16,128,8,128]{3,1,2,0:T(8,128)(2,1)} %bitcast.25) | data formatting | bytes 8388608 | tf_op jit(solution)/shard_map/transpose | solution.py:14
  37.4 0.0 all-gather.3.cloned.1.call-done
  37.4 9.4 %fusion.3 = bf16[2048,1024]{1,0:T(8,128)(2,1)} fusion(bf16[1024,1024]{1,0:T(8,128)(2,1)} %all-gather.3.cloned.1.call-done, bf16[256,8,8,128]{3,2,1,0:T(8,128)(2,1)} %bitcast.26), kind=kOutput, calls=%fused_computation.4 | convolution fusion | flops 4297064448 | bytes 10485760 | tf_op jit(solution)/shard_map/dot_general | solution.py:35
  46.8 0.0 reduce-scatter.2.cloned.1.call-update
  46.8 39.1 %all-gather.5.cloned.1.call-done = bf16[1024,1024]{1,0:T(8,128)(2,1)} async-done(((bf16[128,1024]{1,0:T(8,128)(2,1)}), bf16[1024,1024]{1,0:T(8,128)(2,1)}) %all-gather.5.cloned.1.call-update) | async-done | bytes 2097168 | tf_op jit(solution)/shard_map/all_gather | solution.py:38
  85.9 90.2 %reduce-scatter.2.cloned.1.call-done = bf16[256,1024]{1,0:T(8,128)(2,1)} async-done(((bf16[2048,1024]{1,0:T(8,128)(2,1)}), bf16[256,1024]{1,0:T(8,128)(2,1)}) %reduce-scatter.2.cloned.1.call-update) | async-done | bytes 524304 | tf_op jit(solution)/shard_map/reduce_scatter | solution.py:18
  176.1 3.3 %fusion.6 = bf16[256,1024]{1,0:T(8,128)(2,1)} fusion(bf16[256,1024]{1,0:T(8,128)(2,1)} %reduce-scatter.2.cloned.1.call-done, bf16[1024,1024]{1,0:T(8,128)(2,1)} %all-gather.5.cloned.1.call-done), kind=kOutput, calls=%fused_computation.7 | convolution fusion | flops 537395200 | bytes 3145728 | tf_op jit(solution)/shard_map/dot_general | solution.py:39
  (1 shorter events, 0.0 us)
Async XLA Ops:
  6.5 30.9 %all-gather.3.cloned.1.call-start = ((), (), s32[]{:S(2)}) async-start(), calls=%async_computation.1 | async-start | bytes 2621440 | tf_op jit(solution)/shard_map/all_gather | solution.py:34
  7.3 78.7 %all-gather.5.cloned.1.call-start = ((), (), s32[]{:S(2)}) async-start(), calls=%async_computation.3 | async-start | bytes 2359296 | tf_op jit(solution)/shard_map/all_gather | solution.py:38
  8.0 168.1 %reduce-scatter.2.cloned.1.call-start = ((), (), s32[]{:S(2)}) async-start(), calls=%async_computation.2 | async-start | bytes 4718592 | tf_op jit(solution)/shard_map/reduce_scatter | solution.py:18
Sparse Core Ops, SparseCore 0:
  8.9 25.5 all-gather.2
  36.6 49.2 all-gather.4
  89.6 86.5 reduce-scatter.1
where the time goes:
time: 187 us; the launch traced here: 186 us
  waiting for transfers between devices  131 us (70%)
  other arithmetic  18 us (10%)
  between operations  13.8 us (7%)
  matrix products  12.6 us (7%)
  local copies, waits for them, and re-layouts  10.7 us (6%)
    reduce_scatter x1, waiting for transfers between devices, reduce_whole(): lax.psum_scatter(partial_rows.astype(jnp.bfloat16), 'col', scatter_dimens...  90.2 us
    all_gather x1, waiting for transfers between devices, shards(): full_weight = lax.all_gather(weight, 'col', axis=0, tiled=True)  39.1 us
    scatter-add x1, other arithmetic, densify(): grid = grid.at[tile_rows, tile_cols].add(masked)  15.4 us
    dot_general x1, matrix products, shards(): jnp.dot(dense_block, whole, preferred_element_type=jnp.float32)  9.37 us
    transpose x1, local copies, waits for them, and re-layouts, densify(): grid.transpose(0, 2, 1, 3)  7.67 us
  transfers between devices with their start and end apart: 3, of which 2 were waited for; matrix products, arithmetic and copies ran while one was open for 20% of the time, Pallas kernels for 0%

commit v1 on v0

--- a/solution.py
+++ b/solution.py
@@ -1,7 +1,13 @@
+import functools
+
 import jax
 import jax.numpy as jnp
 from jax import lax
+from jax.experimental import pallas as pl
+from jax.experimental.pallas import tpu as pltpu
 from jax.sharding import PartitionSpec as P
+
+MESH = pl.DeviceIdType.MESH
 
 
 def densify(adjacency_tiles, tile_rows, tile_cols, tile_count, row_blocks, column_blocks):
@@ -40,9 +46,228 @@
     return jnp.maximum(hidden, 0.0).astype(jnp.bfloat16)
 
 
+def layer_kernel(
+    inv, adj_hbm, feat_hbm, w_hbm, out_ref,
+    adj, dense, feat, wfull, psend, own, yr, zr, acc, hidden,
+    lsem, fsend, frecv, wsend, wrecv, vsend, vrecv, ysend, yrecv, zsend, zrecv,
+):
+    p, q = lax.axis_index("row"), lax.axis_index("col")
+    y, z = q % 2, q // 2
+    mate = p + 1 - 2 * (p % 2)
+    across = (p + 2) % 4
+    slots = adj_hbm.shape[0]
+    tb = adj_hbm.shape[1]
+    quarter = wfull.shape[2]
+
+    cp_adj = pltpu.make_async_copy(adj_hbm, adj.at[pl.ds(0, slots)], lsem.at[0])
+    cp_adj.start()
+    cp_feat = pltpu.make_async_copy(feat_hbm, feat.at[0], lsem.at[1])
+    cp_feat.start()
+    w_mine = w_hbm.at[pl.ds(pl.multiple_of(p * quarter, quarter), quarter)]
+    cp_w = pltpu.make_async_copy(w_mine, wfull.at[q, p], lsem.at[2])
+    cp_w.start()
+
+    barrier = pltpu.get_barrier_semaphore()
+    for step in range(1, 8):
+        pl.semaphore_signal(barrier, inc=1, device_id={"col": (q + step) % 8}, device_id_type=MESH)
+    pl.semaphore_signal(barrier, inc=1, device_id={"row": mate}, device_id_type=MESH)
+    pl.semaphore_signal(barrier, inc=1, device_id={"row": across}, device_id_type=MESH)
+    pl.semaphore_wait(barrier, 9)
+
+    def row_copy(src, dst, ssem, rsem, to):
+        return pltpu.make_async_remote_copy(
+            src_ref=src, dst_ref=dst, send_sem=ssem, recv_sem=rsem,
+            device_id={"row": to}, device_id_type=MESH)
+
+    def col_copy(src, dst, ssem, rsem, to):
+        return pltpu.make_async_remote_copy(
+            src_ref=src, dst_ref=dst, send_sem=ssem, recv_sem=rsem,
+            device_id={"col": to}, device_id_type=MESH)
+
+    f_mate = row_copy(feat_hbm, feat.at[1], fsend.at[0], frecv.at[0], mate)
+    f_across = row_copy(feat_hbm, feat.at[2], fsend.at[1], frecv.at[1], across)
+    f_fwd = row_copy(feat.at[2], feat.at[3], fsend.at[2], frecv.at[2], mate)
+    f_mate.start()
+    f_across.start()
+    w_out = [
+        col_copy(w_mine, wfull.at[q, p], wsend.at[step - 1], wrecv.at[step - 1], (q + step) % 8)
+        for step in range(1, 8)
+    ]
+    for copy in w_out:
+        copy.start()
+    v_mate = row_copy(wfull.at[:, p], wfull.at[:, p], vsend.at[0], vrecv.at[0], mate)
+    v_across = row_copy(wfull.at[:, p], wfull.at[:, p], vsend.at[1], vrecv.at[1], across)
+    v_fwd = row_copy(wfull.at[:, across], wfull.at[:, across], vsend.at[2], vrecv.at[2], mate)
+
+    adj[slots] = jnp.zeros((tb, tb), jnp.bfloat16)
+    cp_adj.wait()
+
+    @pl.loop(0, 8)
+    def _(chunk):
+        for half in range(2):
+            for cb in range(8):
+                dense[chunk, half * tb:(half + 1) * tb, cb * tb:(cb + 1) * tb] = adj[
+                    inv[chunk * 16 + half * 8 + cb]]
+
+    power = (1 + 3 * (z % 2)) * (1 + 15 * (z // 2))
+
+    def dest(step):
+        code = 15 * ((3 - step) // 3) + 114 * ((step % 3) % 2) + 153 * ((step % 3) // 2)
+        code = code + 228 * (step // 3)
+        return (code // power) % 4
+
+    def y_copy(k, d):
+        return col_copy(psend.at[k, d], yr.at[k, d], ysend.at[k, d], yrecv.at[k, d], 2 * z + 1 - y)
+
+    def z_copy(k, d):
+        side = (d - z + 4) // 4
+        return col_copy(own.at[k, d], zr.at[side, k, d], zsend.at[k, d], zrecv.at[side, k, d],
+                        q + 4 * side - 2)
+
+    def product(k, chunk):
+        return jnp.dot(dense[chunk], feat[k], preferred_element_type=jnp.float32)
+
+    def compute(k):
+        @pl.loop(0, 4)
+        def _(step):
+            d = dest(step)
+            psend[k, d] = product(k, 2 * d + 1 - y).astype(jnp.bfloat16)
+            y_copy(k, d).start()
+
+        @pl.loop(0, 4)
+        def _(step):
+            d = dest(step)
+            own[k, d] = product(k, 2 * d + y).astype(jnp.bfloat16)
+
+    def reduce(k):
+        @pl.loop(0, 3)
+        def _(step):
+            d = dest(step)
+            side = (d - z + 4) // 4
+            up = z + 1 - 2 * side
+            y_copy(k, d).wait_recv()
+            has_up = (up + 1) % 5 > 0
+
+            @pl.when(has_up)
+            def _():
+                z_copy(k, d).wait_recv()
+                own[k, d] = (own[k, d].astype(jnp.float32) + yr[k, d].astype(jnp.float32)
+                             + zr[side, k, d].astype(jnp.float32)).astype(jnp.bfloat16)
+
+            @pl.when(jnp.logical_not(has_up))
+            def _():
+                own[k, d] = (own[k, d].astype(jnp.float32)
+                             + yr[k, d].astype(jnp.float32)).astype(jnp.bfloat16)
+
+            z_copy(k, d).start()
+
+        y_copy(k, z).wait_recv()
+        acc[...] = own[k, z].astype(jnp.float32) + yr[k, z].astype(jnp.float32)
+
+        for side in (0, 1):
+            @pl.when(z < 3 if side == 0 else z > 0)
+            def _():
+                col_copy(own.at[k, z], zr.at[side, k, z], zsend.at[k, z], zrecv.at[side, k, z],
+                         2 * z + 1 - y).wait_recv()
+                acc[...] += zr[side, k, z].astype(jnp.float32)
+
+    panels = (p, mate, across, (mate + 2) % 4)
+
+    def finish(k):
+        rows = wfull[pl.ds(2 * panels[k], 2)].reshape(8 * quarter, wfull.shape[3])
+        term = jnp.dot(acc[...].astype(jnp.bfloat16), rows, preferred_element_type=jnp.float32)
+        if k == 0:
+            hidden[...] = term
+        elif k < 3:
+            hidden[...] += term
+        else:
+            out_ref[...] = jnp.maximum(hidden[...] + term, 0.0).astype(jnp.bfloat16)
+
+    cp_feat.wait()
+    compute(0)
+    f_mate.wait_recv()
+    compute(1)
+    cp_w.wait()
+    for copy in w_out:
+        copy.wait_recv()
+    f_across.wait_recv()
+    f_fwd.start()
+    v_mate.start()
+    v_across.start()
+    reduce(0)
+    compute(2)
+    v_across.wait_recv()
+    v_fwd.start()
+    v_mate.wait_recv()
+    v_fwd.wait_recv()
+    finish(0)
+    reduce(1)
+    finish(1)
+    f_fwd.wait_recv()
+    compute(3)
+    reduce(2)
+    finish(2)
+    reduce(3)
+    finish(3)
+
+    for copy in [f_mate, f_across, f_fwd, v_mate, v_across, v_fwd] + w_out:
+        copy.wait_send()
+    for k in range(4):
+        @pl.loop(0, 4)
+        def _(step):
+            y_copy(k, dest(step)).wait_send()
+
+        @pl.loop(0, 3)
+        def _(step):
+            z_copy(k, dest(step)).wait_send()
+
+
+def fused_shards(adjacency_tiles, tile_rows, tile_cols, tile_counts, features, weight):
+    tiles = adjacency_tiles[0, 0]
+    slots, tb = tiles.shape[:2]
+    live = jnp.arange(slots, dtype=jnp.int32)
+    key = tile_rows[0, 0] * 8 + tile_cols[0, 0]
+    place = jnp.arange(128, dtype=jnp.int32)
+    hit = (place[:, None] == key[None, :]) & (live[None, :] < tile_counts[0, 0])
+    inv = jnp.min(jnp.where(hit, live[None, :], slots), axis=1)
+    width = features.shape[1]
+    wide = weight.shape[1]
+    bf = jnp.bfloat16
+    dma = pltpu.SemaphoreType.DMA
+    blocks = (4, 4, 256, width)
+    return pl.pallas_call(
+        layer_kernel,
+        out_shape=jax.ShapeDtypeStruct((256, wide), bf),
+        in_specs=[pl.BlockSpec(memory_space=pltpu.SMEM)]
+        + [pl.BlockSpec(memory_space=pl.ANY)] * 3,
+        out_specs=pl.BlockSpec(memory_space=pltpu.VMEM),
+        scratch_shapes=[
+            pltpu.VMEM((slots + 1, tb, tb), bf),
+            pltpu.VMEM((8, 256, 1024), bf),
+            pltpu.VMEM((4, 1024, width), bf),
+            pltpu.VMEM((8, 4, weight.shape[0] // 4, wide), bf),
+            pltpu.VMEM(blocks, bf),
+            pltpu.VMEM(blocks, bf),
+            pltpu.VMEM(blocks, bf),
+            pltpu.VMEM((2,) + blocks, bf),
+            pltpu.VMEM((256, width), jnp.float32),
+            pltpu.VMEM((256, wide), jnp.float32),
+            dma((3,)),
+            dma((3,)), dma((3,)),
+            dma((7,)), dma((7,)),
+            dma((3,)), dma((3,)),
+            dma((4, 4)), dma((4, 4)),
+            dma((4, 4)), dma((2, 4, 4)),
+        ],
+        compiler_params=pltpu.CompilerParams(
+            collective_id=0, has_side_effects=True, vmem_limit_bytes=48 * 2**20),
+    )(inv, tiles, features, weight)
+
+
 def solution(mesh):
+    fits = mesh.shape["row"] == 4 and mesh.shape["col"] == 8
     return jax.shard_map(
-        shards,
+        fused_shards if fits else shards,
         mesh=mesh,
         in_specs=(
             P("row", "col", None, None, None),

time: 187 us -> 89.5 us (0.48)
  waiting for transfers between devices: 131 us -> 0 us
  Pallas kernels: 0 us -> 83.2 us
  other arithmetic: 18 us -> 0.79 us
  between operations: 13.8 us -> 0.68 us
  matrix products: 12.6 us -> 0 us
  local copies, waits for them, and re-layouts: 10.7 us -> 4.52 us
    reduce_scatter x1 -> x0, waiting for transfers between devices: 90.2 us -> none  [reduce_whole(): lax.psum_scatter(partial_rows.astype(jnp.bfloat16), 'col', scatter_dimens...]
    pallas_call x0 -> x1, Pallas kernels: none -> 83.2 us  [fused_shards(): pl.pallas_call(layer_kernel, out_shape=jax.ShapeDtypeStruct((256, wide),...]
    all_gather x2 -> x0, waiting for transfers between devices: 39.1 us -> none  [the longest x1 39.1 us: shards(): full_weight = lax.all_gather(weight, 'col', axis=0, tiled=True)]
    scatter-add x1 -> x0, other arithmetic: 15.4 us -> none  [densify(): grid = grid.at[tile_rows, tile_cols].add(masked)]
    dot_general x2 -> x0, matrix products: 12.6 us -> none  [the longest x1 9.37 us: shards(): jnp.dot(dense_block, whole, preferred_element_type=jnp.float32)]
    transpose x1 -> x0, local copies, waits for them, and re-layouts: 7.67 us -> none  [densify(): grid.transpose(0, 2, 1, 3)]
    unnamed x0 -> x7, local copies, waits for them, and re-layouts: none -> 4.52 us
    broadcast_in_dim x1 -> x0, local copies, waits for them, and re-layouts: 3.02 us -> none  [densify(): jnp.zeros((row_blocks, column_blocks, tile_edge, tile_edge), jnp.bfloat16)]
  transfers between devices with their start and end apart: 3 -> 0, of which waited for: 2 -> 0; matrix products, arithmetic and copies ran while one was open for 20% -> 0% of each run, Pallas kernels for 0% -> 0%
where the time goes in v1:
time: 89.5 us; the launch traced here: 89.2 us
  Pallas kernels  83.2 us (93%)
  local copies, waits for them, and re-layouts  4.52 us (5%)
    pallas_call x1, Pallas kernels, fused_shards(): pl.pallas_call(layer_kernel, out_shape=jax.ShapeDtypeStruct((256, wide),...  83.2 us
    unnamed x7, local copies, waits for them, and re-layouts  4.52 us

profile of v1, /device:TPU:0, one launch (start us, length us, event | category | flops | bytes accessed | tf_op | source)
XLA Modules:
  0.0 89.2 jit_solution(17334767975111482085)
XLA Ops:
  0.7 0.7 add_bitcast_fusion
  1.3 0.1 select_reduce_fusion.inv
  1.4 0.0 copy-start
  1.5 1.7 %copy-done = bf16[1,1,80,128,128]{4,3,2,1,0:T(8,128)(2,1)S(1)} copy-done((bf16[1,1,80,128,128]{4,3,2,1,0:T(8,128)(2,1)S(1)}, bf16[1,1,80,128,128]{4,3,2,1,0:T(8,128)(2,1)}, u32[]{:S(2)}) %copy-start) | copy-done | bytes 2621464
  3.2 0.0 copy-start.1
  3.2 1.0 %copy-done.1 = bf16[1024,256]{1,0:T(8,128)(2,1)S(1)} copy-done((bf16[1024,256]{1,0:T(8,128)(2,1)S(1)}, bf16[1024,256]{1,0:T(8,128)(2,1)}, u32[]{:S(2)}) %copy-start.1) | copy-done | bytes 524312
  4.2 0.0 copy-start.2
  4.2 0.9 %copy-done.2 = bf16[128,1024]{1,0:T(8,128)(2,1)S(1)} copy-done((bf16[128,1024]{1,0:T(8,128)(2,1)S(1)}, bf16[128,1024]{1,0:T(8,128)(2,1)}, u32[]{:S(2)}) %copy-start.2) | copy-done | bytes 262168
  5.2 83.2 %shard_map.64 = bf16[256,1024]{1,0:T(8,128)(2,1)S(1)} custom-call(s32[128]{0:T(128)S(1)} %select_reduce_fusion.inv, bf16[80,128,128]{2,1,0:T(8,128)(2,1)S(1)} %bitcast.5, bf16[1024,256]{1,0:T(8,128)(2,1)S(1)} %copy-done.1, bf16[128,1024]{1,0:T(8,128)(2,1)S(1)} %copy-done.2), custom_call_target="tpu_custom_call" | custom-call | tf_op jit(solution)/shard_map/pallas_call | solution.py:238
  88.4 0.8 copy.9
  (1 shorter events, 0.0 us)
Async XLA Ops:
  1.4 1.7 %copy-start = (bf16[1,1,80,128,128]{4,3,2,1,0:T(8,128)(2,1)S(1)}, bf16[1,1,80,128,128]{4,3,2,1,0:T(8,128)(2,1)}, u32[]{:S(2)}) copy-start(bf16[1,1,80,128,128]{4,3,2,1,0:T(8,128)(2,1)} %param.6) | copy-start | bytes 7864324
  3.2 1.0 %copy-start.1 = (bf16[1024,256]{1,0:T(8,128)(2,1)S(1)}, bf16[1024,256]{1,0:T(8,128)(2,1)}, u32[]{:S(2)}) copy-start(bf16[1024,256]{1,0:T(8,128)(2,1)} %feat_hbm.1) | copy-start | bytes 1572868
  4.2 0.9 %copy-start.2 = (bf16[128,1024]{1,0:T(8,128)(2,1)S(1)}, bf16[128,1024]{1,0:T(8,128)(2,1)}, u32[]{:S(2)}) copy-start(bf16[128,1024]{1,0:T(8,128)(2,1)} %w_hbm.1) | copy-start | bytes 786436

commit v2 on v1

--- a/solution.py
+++ b/solution.py
@@ -112,7 +112,7 @@
     power = (1 + 3 * (z % 2)) * (1 + 15 * (z // 2))
 
     def dest(step):
-        code = 15 * ((3 - step) // 3) + 114 * ((step % 3) % 2) + 153 * ((step % 3) // 2)
+        code = 15 * ((3 - step) // 3) + 90 * ((step % 3) % 2) + 177 * ((step % 3) // 2)
         code = code + 228 * (step // 3)
         return (code // power) % 4
 
@@ -139,28 +139,27 @@
             d = dest(step)
             own[k, d] = product(k, 2 * d + y).astype(jnp.bfloat16)
 
-    def reduce(k):
-        @pl.loop(0, 3)
-        def _(step):
-            d = dest(step)
-            side = (d - z + 4) // 4
-            up = z + 1 - 2 * side
-            y_copy(k, d).wait_recv()
-            has_up = (up + 1) % 5 > 0
-
-            @pl.when(has_up)
-            def _():
-                z_copy(k, d).wait_recv()
-                own[k, d] = (own[k, d].astype(jnp.float32) + yr[k, d].astype(jnp.float32)
-                             + zr[side, k, d].astype(jnp.float32)).astype(jnp.bfloat16)
-
-            @pl.when(jnp.logical_not(has_up))
-            def _():
-                own[k, d] = (own[k, d].astype(jnp.float32)
-                             + yr[k, d].astype(jnp.float32)).astype(jnp.bfloat16)
-
-            z_copy(k, d).start()
-
+    def reduce(k, step):
+        d = dest(step)
+        side = (d - z + 4) // 4
+        up = z + 1 - 2 * side
+        y_copy(k, d).wait_recv()
+        has_up = (up + 1) % 5 > 0
+
+        @pl.when(has_up)
+        def _():
+            z_copy(k, d).wait_recv()
+            own[k, d] = (own[k, d].astype(jnp.float32) + yr[k, d].astype(jnp.float32)
+                         + zr[side, k, d].astype(jnp.float32)).astype(jnp.bfloat16)
+
+        @pl.when(jnp.logical_not(has_up))
+        def _():
+            own[k, d] = (own[k, d].astype(jnp.float32)
+                         + yr[k, d].astype(jnp.float32)).astype(jnp.bfloat16)
+
+        z_copy(k, d).start()
+
+    def settle(k):
         y_copy(k, z).wait_recv()
         acc[...] = own[k, z].astype(jnp.float32) + yr[k, z].astype(jnp.float32)
 
@@ -194,20 +193,31 @@
     f_fwd.start()
     v_mate.start()
     v_across.start()
-    reduce(0)
+    for step in range(3):
+        reduce(0, step)
     compute(2)
     v_across.wait_recv()
     v_fwd.start()
+    reduce(1, 0)
+    settle(0)
     v_mate.wait_recv()
     v_fwd.wait_recv()
     finish(0)
-    reduce(1)
-    finish(1)
+    reduce(1, 1)
+    reduce(1, 2)
     f_fwd.wait_recv()
     compute(3)
-    reduce(2)
+    reduce(2, 0)
+    settle(1)
+    finish(1)
+    reduce(2, 1)
+    reduce(2, 2)
+    reduce(3, 0)
+    settle(2)
     finish(2)
-    reduce(3)
+    reduce(3, 1)
+    reduce(3, 2)
+    settle(3)
     finish(3)
 
     for copy in [f_mate, f_across, f_fwd, v_mate, v_across, v_fwd] + w_out:

time: 89.5 us -> 71.6 us (0.80)
  Pallas kernels: 83.2 us -> 65.3 us
    pallas_call x1, Pallas kernels: 83.2 us -> 65.3 us  [fused_shards(): pl.pallas_call(layer_kernel, out_shape=jax.ShapeDtypeStruct((256, wide),...]
where the time goes in v2:
time: 71.6 us; the launch traced here: 71.3 us
  Pallas kernels  65.3 us (91%)
  local copies, waits for them, and re-layouts  4.52 us (6%)
  other arithmetic  0.79 us (1%)
    pallas_call x1, Pallas kernels, fused_shards(): pl.pallas_call(layer_kernel, out_shape=jax.ShapeDtypeStruct((256, wide),...  65.3 us
    unnamed x7, local copies, waits for them, and re-layouts  4.52 us

profile of v2, /device:TPU:0, one launch (start us, length us, event | category | flops | bytes accessed | tf_op | source)
XLA Modules:
  0.0 71.3 jit_solution(17952260878854251312)
XLA Ops:
  0.7 0.7 add_bitcast_fusion
  1.3 0.1 select_reduce_fusion.inv
  1.4 0.0 copy-start
  1.5 1.7 %copy-done = bf16[1,1,80,128,128]{4,3,2,1,0:T(8,128)(2,1)S(1)} copy-done((bf16[1,1,80,128,128]{4,3,2,1,0:T(8,128)(2,1)S(1)}, bf16[1,1,80,128,128]{4,3,2,1,0:T(8,128)(2,1)}, u32[]{:S(2)}) %copy-start) | copy-done | bytes 2621464
  3.2 0.0 copy-start.1
  3.2 1.0 %copy-done.1 = bf16[1024,256]{1,0:T(8,128)(2,1)S(1)} copy-done((bf16[1024,256]{1,0:T(8,128)(2,1)S(1)}, bf16[1024,256]{1,0:T(8,128)(2,1)}, u32[]{:S(2)}) %copy-start.1) | copy-done | bytes 524312
  4.2 0.0 copy-start.2
  4.2 0.9 %copy-done.2 = bf16[128,1024]{1,0:T(8,128)(2,1)S(1)} copy-done((bf16[128,1024]{1,0:T(8,128)(2,1)S(1)}, bf16[128,1024]{1,0:T(8,128)(2,1)}, u32[]{:S(2)}) %copy-start.2) | copy-done | bytes 262168
  5.2 65.3 %shard_map.64 = bf16[256,1024]{1,0:T(8,128)(2,1)S(1)} custom-call(s32[128]{0:T(128)S(1)} %select_reduce_fusion.inv, bf16[80,128,128]{2,1,0:T(8,128)(2,1)S(1)} %bitcast.5, bf16[1024,256]{1,0:T(8,128)(2,1)S(1)} %copy-done.1, bf16[128,1024]{1,0:T(8,128)(2,1)S(1)} %copy-done.2), custom_call_target="tpu_custom_call" | custom-call | tf_op jit(solution)/shard_map/pallas_call | solution.py:248
  70.5 0.8 %copy.9 = bf16[256,1024]{1,0:T(8,128)(2,1)} copy(bf16[256,1024]{1,0:T(8,128)(2,1)S(1)} %shard_map.64) | data formatting | bytes 1048576
  (1 shorter events, 0.0 us)
Async XLA Ops:
  1.4 1.7 %copy-start = (bf16[1,1,80,128,128]{4,3,2,1,0:T(8,128)(2,1)S(1)}, bf16[1,1,80,128,128]{4,3,2,1,0:T(8,128)(2,1)}, u32[]{:S(2)}) copy-start(bf16[1,1,80,128,128]{4,3,2,1,0:T(8,128)(2,1)} %param.6) | copy-start | bytes 7864324
  3.2 1.0 %copy-start.1 = (bf16[1024,256]{1,0:T(8,128)(2,1)S(1)}, bf16[1024,256]{1,0:T(8,128)(2,1)}, u32[]{:S(2)}) copy-start(bf16[1024,256]{1,0:T(8,128)(2,1)} %feat_hbm.1) | copy-start | bytes 1572868
  4.2 0.9 %copy-start.2 = (bf16[128,1024]{1,0:T(8,128)(2,1)S(1)}, bf16[128,1024]{1,0:T(8,128)(2,1)}, u32[]{:S(2)}) copy-start(bf16[128,1024]{1,0:T(8,128)(2,1)} %w_hbm.1) | copy-start | bytes 786436

commit v3 on v2

--- a/solution.py
+++ b/solution.py
@@ -106,7 +106,7 @@
     def _(chunk):
         for half in range(2):
             for cb in range(8):
-                dense[chunk, half * tb:(half + 1) * tb, cb * tb:(cb + 1) * tb] = adj[
+                dense[chunk % 2, chunk // 2, half * tb:(half + 1) * tb, cb * tb:(cb + 1) * tb] = adj[
                     inv[chunk * 16 + half * 8 + cb]]
 
     power = (1 + 3 * (z % 2)) * (1 + 15 * (z // 2))
@@ -124,20 +124,19 @@
         return col_copy(own.at[k, d], zr.at[side, k, d], zsend.at[k, d], zrecv.at[side, k, d],
                         q + 4 * side - 2)
 
-    def product(k, chunk):
-        return jnp.dot(dense[chunk], feat[k], preferred_element_type=jnp.float32)
+    def product(k, side):
+        rows = dense[side].reshape(4 * dense.shape[2], dense.shape[3])
+        whole = jnp.dot(rows, feat[k], preferred_element_type=jnp.float32)
+        return whole.astype(jnp.bfloat16).reshape(psend.shape[1:])
 
     def compute(k):
+        psend[k] = product(k, 1 - y)
+
         @pl.loop(0, 4)
         def _(step):
-            d = dest(step)
-            psend[k, d] = product(k, 2 * d + 1 - y).astype(jnp.bfloat16)
-            y_copy(k, d).start()
-
-        @pl.loop(0, 4)
-        def _(step):
-            d = dest(step)
-            own[k, d] = product(k, 2 * d + y).astype(jnp.bfloat16)
+            y_copy(k, dest(step)).start()
+
+        own[k] = product(k, y)
 
     def reduce(k, step):
         d = dest(step)
@@ -199,24 +198,24 @@
     v_across.wait_recv()
     v_fwd.start()
     reduce(1, 0)
-    settle(0)
+    f_fwd.wait_recv()
+    compute(3)
+    reduce(1, 1)
+    reduce(1, 2)
     v_mate.wait_recv()
     v_fwd.wait_recv()
+    reduce(2, 0)
+    settle(0)
     finish(0)
-    reduce(1, 1)
-    reduce(1, 2)
-    f_fwd.wait_recv()
-    compute(3)
-    reduce(2, 0)
-    settle(1)
-    finish(1)
     reduce(2, 1)
     reduce(2, 2)
     reduce(3, 0)
+    settle(1)
+    finish(1)
+    reduce(3, 1)
+    reduce(3, 2)
     settle(2)
     finish(2)
-    reduce(3, 1)
-    reduce(3, 2)
     settle(3)
     finish(3)
 
@@ -253,7 +252,7 @@
         out_specs=pl.BlockSpec(memory_space=pltpu.VMEM),
         scratch_shapes=[
             pltpu.VMEM((slots + 1, tb, tb), bf),
-            pltpu.VMEM((8, 256, 1024), bf),
+            pltpu.VMEM((2, 4, 256, 1024), bf),
             pltpu.VMEM((4, 1024, width), bf),
             pltpu.VMEM((8, 4, weight.shape[0] // 4, wide), bf),
             pltpu.VMEM(blocks, bf),

time: 71.6 us -> 71.3 us (level)
  no operation moved by 1% of the time
where the time goes in v3:
time: 71.3 us; the launch traced here: 71 us
  Pallas kernels  65 us (91%)
  local copies, waits for them, and re-layouts  4.52 us (6%)
  other arithmetic  0.79 us (1%)
    pallas_call x1, Pallas kernels, fused_shards(): pl.pallas_call(layer_kernel, out_shape=jax.ShapeDtypeStruct((256, wide),...  65 us
    unnamed x7, local copies, waits for them, and re-layouts  4.52 us

profile of v3, /device:TPU:0, one launch (start us, length us, event | category | flops | bytes accessed | tf_op | source)
XLA Modules:
  0.0 71.0 jit_solution(2725422081034577567)
XLA Ops:
  0.7 0.7 add_bitcast_fusion
  1.3 0.1 select_reduce_fusion.inv
  1.4 0.0 copy-start
  1.5 1.7 %copy-done = bf16[1,1,80,128,128]{4,3,2,1,0:T(8,128)(2,1)S(1)} copy-done((bf16[1,1,80,128,128]{4,3,2,1,0:T(8,128)(2,1)S(1)}, bf16[1,1,80,128,128]{4,3,2,1,0:T(8,128)(2,1)}, u32[]{:S(2)}) %copy-start) | copy-done | bytes 2621464
  3.2 0.0 copy-start.1
  3.2 1.0 %copy-done.1 = bf16[1024,256]{1,0:T(8,128)(2,1)S(1)} copy-done((bf16[1024,256]{1,0:T(8,128)(2,1)S(1)}, bf16[1024,256]{1,0:T(8,128)(2,1)}, u32[]{:S(2)}) %copy-start.1) | copy-done | bytes 524312
  4.2 0.0 copy-start.2
  4.2 0.9 %copy-done.2 = bf16[128,1024]{1,0:T(8,128)(2,1)S(1)} copy-done((bf16[128,1024]{1,0:T(8,128)(2,1)S(1)}, bf16[128,1024]{1,0:T(8,128)(2,1)}, u32[]{:S(2)}) %copy-start.2) | copy-done | bytes 262168
  5.2 65.0 %shard_map.64 = bf16[256,1024]{1,0:T(8,128)(2,1)S(1)} custom-call(s32[128]{0:T(128)S(1)} %select_reduce_fusion.inv, bf16[80,128,128]{2,1,0:T(8,128)(2,1)S(1)} %bitcast.5, bf16[1024,256]{1,0:T(8,128)(2,1)S(1)} %copy-done.1, bf16[128,1024]{1,0:T(8,128)(2,1)S(1)} %copy-done.2), custom_call_target="tpu_custom_call" | custom-call | tf_op jit(solution)/shard_map/pallas_call | solution.py:247
  70.2 0.8 %copy.9 = bf16[256,1024]{1,0:T(8,128)(2,1)} copy(bf16[256,1024]{1,0:T(8,128)(2,1)S(1)} %shard_map.64) | data formatting | bytes 1048576
  (1 shorter events, 0.0 us)
Async XLA Ops:
  1.4 1.7 %copy-start = (bf16[1,1,80,128,128]{4,3,2,1,0:T(8,128)(2,1)S(1)}, bf16[1,1,80,128,128]{4,3,2,1,0:T(8,128)(2,1)}, u32[]{:S(2)}) copy-start(bf16[1,1,80,128,128]{4,3,2,1,0:T(8,128)(2,1)} %param.6) | copy-start | bytes 7864324
  3.2 1.0 %copy-start.1 = (bf16[1024,256]{1,0:T(8,128)(2,1)S(1)}, bf16[1024,256]{1,0:T(8,128)(2,1)}, u32[]{:S(2)}) copy-start(bf16[1024,256]{1,0:T(8,128)(2,1)} %feat_hbm.1) | copy-start | bytes 1572868
  4.2 0.9 %copy-start.2 = (bf16[128,1024]{1,0:T(8,128)(2,1)S(1)}, bf16[128,1024]{1,0:T(8,128)(2,1)}, u32[]{:S(2)}) copy-start(bf16[128,1024]{1,0:T(8,128)(2,1)} %w_hbm.1) | copy-start | bytes 786436

commit v4 on v3

--- a/solution.py
+++ b/solution.py
@@ -102,12 +102,13 @@
     adj[slots] = jnp.zeros((tb, tb), jnp.bfloat16)
     cp_adj.wait()
 
-    @pl.loop(0, 8)
-    def _(chunk):
-        for half in range(2):
-            for cb in range(8):
-                dense[chunk % 2, chunk // 2, half * tb:(half + 1) * tb, cb * tb:(cb + 1) * tb] = adj[
-                    inv[chunk * 16 + half * 8 + cb]]
+    def place(side):
+        @pl.loop(0, 4)
+        def _(d):
+            for half in range(2):
+                for cb in range(8):
+                    dense[side, d, half * tb:(half + 1) * tb, cb * tb:(cb + 1) * tb] = adj[
+                        inv[(2 * d + side) * 16 + half * 8 + cb]]
 
     power = (1 + 3 * (z % 2)) * (1 + 15 * (z // 2))
 
@@ -130,11 +131,21 @@
         return whole.astype(jnp.bfloat16).reshape(psend.shape[1:])
 
     def compute(k):
-        psend[k] = product(k, 1 - y)
-
-        @pl.loop(0, 4)
-        def _(step):
-            y_copy(k, dest(step)).start()
+        if k == 0:
+            @pl.loop(0, 4)
+            def _(step):
+                d = dest(step)
+                psend[k, d] = jnp.dot(dense[1 - y, d], feat[k],
+                                      preferred_element_type=jnp.float32).astype(jnp.bfloat16)
+                y_copy(k, d).start()
+
+            place(y)
+        else:
+            psend[k] = product(k, 1 - y)
+
+            @pl.loop(0, 4)
+            def _(step):
+                y_copy(k, dest(step)).start()
 
         own[k] = product(k, y)
 
@@ -181,6 +192,7 @@
         else:
             out_ref[...] = jnp.maximum(hidden[...] + term, 0.0).astype(jnp.bfloat16)
 
+    place(1 - y)
     cp_feat.wait()
     compute(0)
     f_mate.wait_recv()

time: 71.3 us -> 71.7 us (level)
  no operation moved by 1% of the time
where the time goes in v4:
time: 71.7 us; the launch traced here: 71.4 us
  Pallas kernels  65.5 us (91%)
  local copies, waits for them, and re-layouts  4.52 us (6%)
  other arithmetic  0.79 us (1%)
    pallas_call x1, Pallas kernels, fused_shards(): pl.pallas_call(layer_kernel, out_shape=jax.ShapeDtypeStruct((256, wide),...  65.5 us
    unnamed x7, local copies, waits for them, and re-layouts  4.52 us

profile of v4, /device:TPU:0, one launch (start us, length us, event | category | flops | bytes accessed | tf_op | source)
XLA Modules:
  0.0 71.4 jit_solution(5244495828888807633)
XLA Ops:
  0.7 0.7 add_bitcast_fusion
  1.3 0.1 select_reduce_fusion.inv
  1.4 0.0 copy-start
  1.5 1.7 %copy-done = bf16[1,1,80,128,128]{4,3,2,1,0:T(8,128)(2,1)S(1)} copy-done((bf16[1,1,80,128,128]{4,3,2,1,0:T(8,128)(2,1)S(1)}, bf16[1,1,80,128,128]{4,3,2,1,0:T(8,128)(2,1)}, u32[]{:S(2)}) %copy-start) | copy-done | bytes 2621464
  3.2 0.0 copy-start.1
  3.2 1.0 %copy-done.1 = bf16[1024,256]{1,0:T(8,128)(2,1)S(1)} copy-done((bf16[1024,256]{1,0:T(8,128)(2,1)S(1)}, bf16[1024,256]{1,0:T(8,128)(2,1)}, u32[]{:S(2)}) %copy-start.1) | copy-done | bytes 524312
  4.2 0.0 copy-start.2
  4.2 0.9 %copy-done.2 = bf16[128,1024]{1,0:T(8,128)(2,1)S(1)} copy-done((bf16[128,1024]{1,0:T(8,128)(2,1)S(1)}, bf16[128,1024]{1,0:T(8,128)(2,1)}, u32[]{:S(2)}) %copy-start.2) | copy-done | bytes 262168
  5.2 65.5 %shard_map.64 = bf16[256,1024]{1,0:T(8,128)(2,1)S(1)} custom-call(s32[128]{0:T(128)S(1)} %select_reduce_fusion.inv, bf16[80,128,128]{2,1,0:T(8,128)(2,1)S(1)} %bitcast.5, bf16[1024,256]{1,0:T(8,128)(2,1)S(1)} %copy-done.1, bf16[128,1024]{1,0:T(8,128)(2,1)S(1)} %copy-done.2), custom_call_target="tpu_custom_call" | custom-call | tf_op jit(solution)/shard_map/pallas_call | solution.py:259
  70.7 0.8 %copy.9 = bf16[256,1024]{1,0:T(8,128)(2,1)} copy(bf16[256,1024]{1,0:T(8,128)(2,1)S(1)} %shard_map.64) | data formatting | bytes 1048576
  (1 shorter events, 0.0 us)
Async XLA Ops:
  1.4 1.7 %copy-start = (bf16[1,1,80,128,128]{4,3,2,1,0:T(8,128)(2,1)S(1)}, bf16[1,1,80,128,128]{4,3,2,1,0:T(8,128)(2,1)}, u32[]{:S(2)}) copy-start(bf16[1,1,80,128,128]{4,3,2,1,0:T(8,128)(2,1)} %param.6) | copy-start | bytes 7864324
  3.2 1.0 %copy-start.1 = (bf16[1024,256]{1,0:T(8,128)(2,1)S(1)}, bf16[1024,256]{1,0:T(8,128)(2,1)}, u32[]{:S(2)}) copy-start(bf16[1024,256]{1,0:T(8,128)(2,1)} %feat_hbm.1) | copy-start | bytes 1572868
  4.2 0.9 %copy-start.2 = (bf16[128,1024]{1,0:T(8,128)(2,1)S(1)}, bf16[128,1024]{1,0:T(8,128)(2,1)}, u32[]{:S(2)}) copy-start(bf16[128,1024]{1,0:T(8,128)(2,1)} %w_hbm.1) | copy-start | bytes 786436
